TPU v7x, 256 devices: a whole 4x4x8 slice. The times are simulated.
256 devices in a mesh: dp: 16 (over z, core), expert: 16 (over y, x).
Axes of the slice: x: 4, y: 4, z: 8, core: 2. Of those that a mesh axis runs over, the one named last changes fastest.
Arguments:
- cotangent: bfloat16 [32768, 2048], P(('dp', 'expert')), may hold values from -6 to 6
- saved_gate_up: bfloat16 [32768, 8, 1536], P(('dp', 'expert')), may hold values from -6 to 6
- route_ids: int32 [32768, 8], P(('dp', 'expert')), may hold values from 0 to 31, all different within a row; in each aligned block of 128 rows (0 to 127, 128 to 255, ...) at most 64 rows name the same one
- route_weights: float32 [32768, 8], P(('dp', 'expert')), may hold values from 0.05 to 1
- w_down: bfloat16 [32, 768, 2048], P('expert', 'dp'), may hold values from -0.21875 to 0.21875
Outputs:
- grad_gate_up: bfloat16 [32768, 8, 1536], P(('dp', 'expert'))
- route_grad: float32 [32768, 8], P(('dp', 'expert'))
- grad_down: float32 [32, 768, 2048], P('expert', 'dp')
Inputs may be any that keep to these rules, and one draw needn't show every extreme that they name: `route_ids`: within the rows of one device (aligned blocks of 128 tokens), no expert is named by more than 64 routes, and in every draw some expert is named by exactly 64; the 8 experts of a token are distinct.
All inputs are finite; a program needn't handle non-finite values.
Results may differ from a plain program's by a relative error of at most 0.02.
Values may be sent and summed in bfloat16 or wider, within the bound.
A program may use at most 128 MiB of HBM per device.

v0:
```python
import jax
import jax.numpy as jnp
from jax import lax
from jax.sharding import PartitionSpec as P


def slot_counts(ids, experts):
    routes = ids.shape[-1]
    onehot = (ids[..., None] == jnp.arange(experts, dtype=jnp.int32)).astype(jnp.bfloat16)
    lower = (jnp.arange(routes)[:, None] > jnp.arange(routes)[None, :]).astype(jnp.bfloat16)
    before = jnp.einsum("rq,...qe->...re", lower, onehot, preferred_element_type=jnp.float32)
    return jnp.sum(before * onehot.astype(jnp.float32), axis=-1).astype(jnp.int32)


def local(cotangent, saved_gate_up, route_ids, route_weights, w_down):
    tokens, top = route_ids.shape
    width = cotangent.shape[1]
    hidden_units = saved_gate_up.shape[2] // 2
    owners = lax.axis_size("expert")
    replicas = lax.axis_size("dp")
    me = lax.axis_index("expert")
    local_experts = w_down.shape[0]
    experts = local_experts * owners
    capacity = min(tokens, 2 * tokens * top // experts)
    routes = tokens * top
    cot_group = lax.all_gather(cotangent, "expert", axis=0, tiled=True)
    ids_group = lax.all_gather(route_ids.reshape(1, routes), "expert", axis=0, tiled=True)
    full_down = lax.all_gather(w_down, "dp", axis=1, tiled=True)
    gate = saved_gate_up[:, :, :hidden_units].astype(jnp.float32)
    up = saved_gate_up[:, :, hidden_units:].astype(jnp.float32)
    sig = jax.nn.sigmoid(gate)
    act = gate * sig
    hidden = (act * up).astype(jnp.bfloat16)
    weights = route_weights[:, :, None]
    scaled = (weights * hidden.astype(jnp.float32)).astype(jnp.bfloat16)
    flat_ids = route_ids.reshape(routes)
    slot = slot_counts(flat_ids, experts)
    position = flat_ids * capacity + slot
    slot_ids = jnp.arange(experts * capacity, dtype=jnp.int32)
    match = position[None, :] == slot_ids[:, None]
    route_of_slot = jnp.sum(
        jnp.where(match, jnp.arange(routes, dtype=jnp.int32)[None, :], 0), axis=1
    )
    filled = jnp.any(match, axis=1)
    h_rows = jnp.where(
        filled[:, None],
        scaled.reshape(routes, hidden_units)[route_of_slot],
        jnp.zeros((), jnp.bfloat16),
    )
    h_send = h_rows.reshape(owners, local_experts, capacity, hidden_units)
    slot_all = slot_counts(ids_group, experts)
    mine = me * local_experts + jnp.arange(local_experts, dtype=jnp.int32)
    pos_all = ids_group * capacity + slot_all
    want = (mine[:, None] * capacity + jnp.arange(capacity, dtype=jnp.int32)[None, :]).reshape(-1)
    hit = pos_all[:, None, :] == want[None, :, None]
    token_of = jnp.sum(
        jnp.where(hit, (jnp.arange(routes, dtype=jnp.int32) // top)[None, None, :], 0), axis=2
    )
    rows = (jnp.arange(owners, dtype=jnp.int32)[:, None] * tokens + token_of).reshape(
        owners, local_experts, capacity
    )
    rows = jnp.transpose(rows, (1, 0, 2)).reshape(local_experts, owners * capacity)
    dy_recv = cot_group[rows]
    h_recv = lax.all_to_all(h_send, "expert", split_axis=0, concat_axis=2, tiled=True)[0]
    grads = jnp.einsum(
        "jsd,jfd->jsf", dy_recv, full_down, preferred_element_type=jnp.float32
    ).astype(jnp.bfloat16)
    back = lax.all_to_all(
        grads.reshape(1, local_experts, owners * capacity, hidden_units),
        "expert",
        split_axis=2,
        concat_axis=0,
        tiled=True,
    )
    parts = []
    for j in range(local_experts):
        part = jnp.einsum(
            "sf,sd->fd", h_recv[j], dy_recv[j], preferred_element_type=jnp.float32
        ).astype(jnp.bfloat16)
        parts.append(
            lax.psum_scatter(part, "dp", scatter_dimension=0, tiled=True).astype(jnp.float32)
        )
    grad_down = jnp.stack(parts)
    returned_rows = back.reshape(experts * capacity, hidden_units)[position]
    qf = returned_rows.reshape(tokens, top, hidden_units).astype(jnp.float32)
    route_grad = jnp.sum(qf * hidden.astype(jnp.float32), -1)
    d_hidden = weights * qf
    d_gate = d_hidden * up * sig * (1.0 + gate * (1.0 - sig))
    d_up = d_hidden * act
    grad_gate_up = jnp.concatenate([d_gate, d_up], -1).astype(jnp.bfloat16)
    return (grad_gate_up, route_grad, grad_down)


def solution(mesh):
    return jax.shard_map(
        local,
        mesh=mesh,
        in_specs=(
            P(("dp", "expert"), None),
            P(("dp", "expert"), None, None),
            P(("dp", "expert"), None),
            P(("dp", "expert"), None),
            P("expert", "dp", None),
        ),
        out_specs=(
            P(("dp", "expert"), None, None),
            P(("dp", "expert"), None),
            P("expert", "dp", None),
        ),
        check_vma=False,
    )
```

profile of v0, /device:TPU:2, one launch (start us, length us, event | category | flops | bytes accessed | tf_op | source)
XLA Modules:
  0.0 409.4 jit_solution(11496074652841021074)
XLA Ops:
  7.2 0.0 all-gather.4.cloned.1.call-start
  7.2 0.7 all-gather.4.cloned.1.call-update
  7.9 0.0 all-gather.6.cloned.1.call-start
  7.9 0.7 all-gather.6.cloned.1.call-update
  8.7 0.8 copy.30
  9.4 0.1 reshape.205
  9.5 23.6 %all-gather = s32[16,1,1024]{2,1,0:T(1,128)S(1)} all-gather(s32[1,1,1024]{2,1,0:T(1,128)S(1)} %reshape.205), channel_id=1, replica_groups=mesh['dp'=16,'expert'=16] {'expert'}, dimensions={0}, use_global_device_ids=true | all-gather | bytes 69632 | tf_op jit(solution)/shard_map/all_gather | solution.py:27
  33.2 0.1 iota_add_fusion
  33.3 0.1 add.119
  33.4 1.4 fusion.27
  34.8 1.0 select_reduce_fusion.1
  35.8 0.1 reduce_sum.51
  35.9 0.1 add_bitcast_fusion
  36.0 0.1 reshape.171
  36.1 53.2 %all-gather.4.cloned.1.call-done = bf16[2048,2048]{1,0:T(8,128)(2,1)} async-done(((bf16[128,2048]{1,0:T(8,128)(2,1)}), bf16[2048,2048]{1,0:T(8,128)(2,1)}) %all-gather.4.cloned.1.call-update) | async-done | bytes 8388624 | tf_op jit(solution)/shard_map/all_gather | solution.py:26
  89.3 20.8 %gather_fusion = bf16[2048,2048]{1,0:T(8,128)(2,1)} fusion(bf16[2048,2048]{1,0:T(8,128)(2,1)} %all-gather.4.cloned.1.call-done, s32[2048]{0:T(1024)S(1)} %bitcast_clamp_fusion), kind=kCustom, calls=%fused_computation | custom fusion | bytes 16785408 | tf_op jit(solution)/shard_map/gather | solution.py:63
  110.1 26.9 %all-gather.6.cloned.1.call-done = bf16[2,768,2048]{2,1,0:T(8,128)(2,1)} async-done(((bf16[2,48,2048]{2,1,0:T(8,128)(2,1)}), bf16[2,768,2048]{2,1,0:T(8,128)(2,1)}) %all-gather.6.cloned.1.call-update) | async-done | bytes 6291472 | tf_op jit(solution)/shard_map/all_gather | solution.py:28
  136.9 11.0 %convert_bitcast_fusion = bf16[1,2,1024,768]{3,2,1,0:T(8,128)(2,1)S(1)} fusion(bf16[2,1024,2048]{2,1,0:T(8,128)(2,1)} %bitcast.55, bf16[2,768,2048]{2,1,0:T(8,128)(2,1)} %all-gather.6.cloned.1.call-done), kind=kOutput, calls=%fused_computation.38 | convolution fusion | flops 6444023808 | bytes 17825792 | tf_op jit(solution)/shard_map/jsd,jfd->jsf/dot_general | solution.py:65
  147.9 4.9 %copy.32 = bf16[1,2,1024,768]{3,1,0,2:T(2,128)(2,1)} copy(bf16[1,2,1024,768]{3,2,1,0:T(8,128)(2,1)S(1)} %convert_bitcast_fusion) | data formatting | bytes 6291456 | tf_op jit(solution)/shard_map/reshape | solution.py:69
  152.8 7.4 %all-to-all-start = ((bf16[1,2,1024,768]{3,1,0,2:T(2,128)(2,1)}), bf16[1,2,1024,768]{3,1,0,2:T(2,128)(2,1)S(1)}, u32[]{:S(2)}, u32[]{:S(2)}) async-start(bf16[1,2,1024,768]{3,1,0,2:T(2,128)(2,1)} %copy.32), calls=%async_computation | async-start | bytes 6291456 | tf_op jit(solution)/shard_map/all_to_all | solution.py:68
  160.2 0.0 reduce-scatter.5.cloned.1.call-start
  160.3 0.1 eq.60
  160.4 0.1 copy.29
  160.5 0.1 copy.34
  160.6 0.1 mul.102
  160.7 0.5 fusion.31
  161.3 1.0 fusion
  162.3 0.1 broadcast_in_dim.36
  162.4 0.9 select_reduce_fusion
  163.4 41.3 %all-to-all-done = bf16[1,2,1024,768]{3,1,0,2:T(2,128)(2,1)S(1)} async-done(((bf16[1,2,1024,768]{3,1,0,2:T(2,128)(2,1)}), bf16[1,2,1024,768]{3,1,0,2:T(2,128)(2,1)S(1)}, u32[]{:S(2)}, u32[]{:S(2)}) %all-to-all-start) | async-done | bytes 3145760 | tf_op jit(solution)/shard_map/all_to_all | solution.py:68
  204.7 1.7 copy-done.1
  206.3 2.5 copy.33
  208.9 5.2 %gather_fusion.1 = bf16[1024,768]{1,0:T(8,128)(2,1)} fusion(bf16[2048,768]{1,0:T(8,128)(2,1)S(1)} %bitcast.51, s32[1024]{0:T(1024)S(1)} %broadcast_clamp_fusion.1), kind=kCustom, calls=%fused_computation.1 | custom fusion | bytes 3149824 | tf_op jit(solution)/shard_map/gather | solution.py:84
  214.1 5.0 %fusion.29 = (bf16[1024,768]{1,0:T(8,128)(2,1)S(1)}, bf16[128,8,768]{2,1,0:T(8,128)(2,1)S(1)}, bf16[128,8,768]{2,1,0:T(8,128)(2,1)}, bf16[128,8,768]{2,1,0:T(8,128)(2,1)}) fusion(f32[128,8]{1,0:T(8,128)S(1)} %copy.29, bf16[128,8,1536]{2,1,0:T(8,128)(2,1)} %param.6, bf16[1024,768]{1,0:T(8,128)(2,1)} %gather_fusion.1), kind=kLoop, calls=%fused_computation.44 | loop fusion | flops 17301504 | bytes 11014144 | tf_op jit(solution)/shard_map/reshape | solution.py:47
  219.0 9.4 %gather_fusion.2 = bf16[2048,768]{1,0:T(8,128)(2,1)} fusion(bf16[1024,768]{1,0:T(8,128)(2,1)S(1)} %get-tuple-element.9, s32[2048]{0:T(1024)S(1)} %broadcast_clamp_fusion), kind=kCustom, calls=%fused_computation.2 | custom fusion | bytes 6299648 | tf_op jit(solution)/shard_map/gather | solution.py:47
  228.4 2.3 broadcast_select_fusion
  230.7 46.5 %all_to_all.30 = bf16[16,2,64,768]{3,2,1,0:T(8,128)(2,1)S(1)} all-to-all(bf16[16,2,64,768]{3,2,1,0:T(8,128)(2,1)S(1)} %broadcast_select_fusion), channel_id=1, replica_groups=mesh['dp'=16,'expert'=16] {'expert'}, dimensions={0} | all-to-all | bytes 6291456 | tf_op jit(solution)/shard_map/all_to_all | solution.py:64
  277.2 0.2 fusion.42
  277.5 4.9 %fusion.13 = bf16[768,2048]{1,0:T(8,128)(2,1)} fusion(bf16[1024,768]{1,0:T(8,128)(2,1)S(1)} %bitcast.59, bf16[2048,2048]{1,0:T(8,128)(2,1)S(1)} %bitcast.57), kind=kOutput, calls=%fused_computation.25 | convolution fusion | flops 3222798336 | bytes 8912896 | tf_op jit(solution)/shard_map/sf,sd->fd/dot_general | solution.py:77
  282.4 0.0 reduce-scatter.3.cloned.1.call-start
  282.5 7.0 %fusion.10 = bf16[768,2048]{1,0:T(8,128)(2,1)} fusion(bf16[1024,768]{1,0:T(8,128)(2,1)S(1)} %bitcast.58, bf16[2048,2048]{1,0:T(8,128)(2,1)} %gather_fusion), kind=kOutput, calls=%fused_computation.24 | convolution fusion | flops 3222798336 | bytes 8912896 | tf_op jit(solution)/shard_map/sf,sd->fd/dot_general | solution.py:77
  289.6 1.4 copy-done
  290.9 0.5 fusion.22
  291.4 0.7 copy.36
  292.1 3.8 pad_maximum_fusion
  295.9 43.3 %reduce-scatter.5.cloned.1.call-done = bf16[48,2048]{1,0:T(8,128)(2,1)} async-done(((bf16[768,2048]{1,0:T(8,128)(2,1)}), bf16[48,2048]{1,0:T(8,128)(2,1)}) %reduce-scatter.5.cloned.1.call-update) | async-done | bytes 196624 | tf_op jit(solution)/shard_map/reduce_scatter | solution.py:81
  339.2 61.7 %reduce-scatter.3.cloned.1.call-done = bf16[48,2048]{1,0:T(8,128)(2,1)} async-done(((bf16[768,2048]{1,0:T(8,128)(2,1)}), bf16[48,2048]{1,0:T(8,128)(2,1)}) %reduce-scatter.3.cloned.1.call-update) | async-done | bytes 196624 | tf_op jit(solution)/shard_map/reduce_scatter | solution.py:81
  400.9 2.0 maximum_convert_fusion
  (28 shorter events, 0.2 us)
Async XLA Ops:
  7.2 82.1 %all-gather.4.cloned.1.call-start = ((), (), s32[]{:S(2)}) async-start(), calls=%async_computation.4 | async-start | bytes 8912896 | tf_op jit(solution)/shard_map/all_gather | solution.py:26
  7.9 129.0 %all-gather.6.cloned.1.call-start = ((), (), s32[]{:S(2)}) async-start(), calls=%async_computation.5 | async-start | bytes 6684672 | tf_op jit(solution)/shard_map/all_gather | solution.py:28
  152.8 7.5 %copy-start.3 = (f32[128,8]{0,1:T(8,128)S(1)}, f32[128,8]{0,1:T(8,128)}, u32[]{:S(2)}) copy-start(f32[128,8]{0,1:T(8,128)} %param.8) | copy-start | bytes 12292
  152.8 7.7 %copy-start.2 = (s32[128,8]{0,1:T(8,128)S(1)}, s32[128,8]{0,1:T(8,128)}, u32[]{:S(2)}) copy-start(s32[128,8]{0,1:T(8,128)} %param.7) | copy-start | bytes 12292
  152.8 51.8 %all-to-all-start = ((bf16[1,2,1024,768]{3,1,0,2:T(2,128)(2,1)}), bf16[1,2,1024,768]{3,1,0,2:T(2,128)(2,1)S(1)}, u32[]{:S(2)}, u32[]{:S(2)}) async-start(bf16[1,2,1024,768]{3,1,0,2:T(2,128)(2,1)} %copy.32), calls=%async_computation | async-start | bytes 6291456 | tf_op jit(solution)/shard_map/all_to_all | solution.py:68
  160.2 179.0 %reduce-scatter.5.cloned.1.call-start = ((), (), s32[]{:S(2)}) async-start(), calls=%async_computation.7 | async-start | bytes 3342336 | tf_op jit(solution)/shard_map/reduce_scatter | solution.py:81
  204.7 1.7 copy-start.1
  228.4 49.1 %slice-start = ((s8[8388608]{0:T(1024)(128)(4,1)}), s8[4194304]{0:T(1024)(128)(4,1)S(1)}, s32[]{:S(2)}) async-start(s8[8388608]{0:T(1024)(128)(4,1)} %bitcast.56), calls=%async_computation.8 | async-start | bytes 8388608
  230.7 46.8 %slice-start.1 = ((s8[8388608]{0:T(1024)(128)(4,1)}), s8[4194304]{0:T(1024)(128)(4,1)S(1)}, s32[]{:S(2)}) async-start(s8[8388608]{0:T(1024)(128)(4,1)} %bitcast.56), calls=%async_computation.9 | async-start | bytes 8388608
  282.4 118.5 %reduce-scatter.3.cloned.1.call-start = ((), (), s32[]{:S(2)}) async-start(), calls=%async_computation.6 | async-start | bytes 3342336 | tf_op jit(solution)/shard_map/reduce_scatter | solution.py:81
  289.5 1.4 copy-start
Sparse Core Ops, SparseCore 0:
  10.4 78.7 all-gather.3
  91.1 45.7 all-gather.5
  282.6 56.6 reduce-scatter.4
  341.6 59.2 reduce-scatter.2
where the time goes:
time: 410 us; the launch traced here: 409 us
  waiting for transfers between devices  228 us (56%)
  blocking collectives  70.2 us (17%)
  local copies, waits for them, and re-layouts  48.4 us (12%)
  matrix products  24.9 us (6%)
  other arithmetic  16.6 us (4%)
  between operations  14 us (3%)
  starting transfers between devices  7.56 us (2%)
    reduce_scatter x2, waiting for transfers between devices, local(): lax.psum_scatter(part, 'dp', scatter_dimension=0, tiled=True)  105 us
    all_gather x1, waiting for transfers between devices, local(): cot_group = lax.all_gather(cotangent, 'expert', axis=0, tiled=True)  53.2 us
    all_to_all x1, blocking collectives, local(): lax.all_to_all(h_send, 'expert', split_axis=0, concat_axis=2, tiled=True)[0]  46.5 us
    all_to_all x1, waiting for transfers between devices, local(): lax.all_to_all(grads.reshape(1, local_experts, owners * capacity, hidden_...  41.3 us
    all_gather x1, waiting for transfers between devices, local(): full_down = lax.all_gather(w_down, 'dp', axis=1, tiled=True)  26.9 us
    all_gather x1, blocking collectives, local(): lax.all_gather(route_ids.reshape(1, routes), 'expert', axis=0, tiled=True)  23.6 us
    gather x1, local copies, waits for them, and re-layouts, local(): dy_recv = cot_group[rows]  20.8 us
    dot_general x2, matrix products, local(): jnp.einsum('sf,sd->fd', h_recv[j], dy_recv[j], preferred_element_type=jnp...  11.9 us
  transfers between devices with their start and end apart: 5, of which 5 were waited for; matrix products, arithmetic and copies ran while one was open for 10% of the time, Pallas kernels for 0%

commit v1 on v0

--- a/solution.py
+++ b/solution.py
@@ -2,6 +2,17 @@
 import jax.numpy as jnp
 from jax import lax
 from jax.sharding import PartitionSpec as P
+
+
+def gather_by_hops(x, axis, dim):
+    size = lax.axis_size(axis)
+    forward = [(i, (i + 1) % size) for i in range(size)]
+    terms = [x]
+    for far in range(1, size):
+        terms = [lax.ppermute(terms[0], axis, forward), *terms]
+    full = jnp.concatenate(terms, axis=dim)
+    turn = (lax.axis_index(axis) + 1) * terms[-1].shape[dim]
+    return jnp.roll(full, turn, axis=dim)
 
 
 def slot_counts(ids, experts):
@@ -25,7 +36,7 @@
     routes = tokens * top
     cot_group = lax.all_gather(cotangent, "expert", axis=0, tiled=True)
     ids_group = lax.all_gather(route_ids.reshape(1, routes), "expert", axis=0, tiled=True)
-    full_down = lax.all_gather(w_down, "dp", axis=1, tiled=True)
+    full_down = gather_by_hops(w_down, "dp", 1)
     gate = saved_gate_up[:, :, :hidden_units].astype(jnp.float32)
     up = saved_gate_up[:, :, hidden_units:].astype(jnp.float32)
     sig = jax.nn.sigmoid(gate)

time: 410 us -> 476 us (1.16)
  local copies, waits for them, and re-layouts: 48.4 us -> 88.2 us
  waiting for transfers between devices: 228 us -> 259 us
  blocking collectives: 70.2 us -> 62.8 us
    ppermute x0 -> x15, waiting for transfers between devices: none -> 114 us  [gather_by_hops(): terms = [lax.ppermute(terms[0], axis, forward), *terms]]
    all_gather x1, waiting for transfers between devices: 53.2 us -> 0.01 us  [local(): cot_group = lax.all_gather(cotangent, 'expert', axis=0, tiled=True)]
    unnamed x17 -> x62, local copies, waits for them, and re-layouts: 4.74 us -> 40.9 us
    all_gather x1 -> x0, waiting for transfers between devices: 26.9 us -> none  [local(): full_down = lax.all_gather(w_down, 'dp', axis=1, tiled=True)]
    all_to_all x1, waiting for transfers between devices: 41.3 us -> 31.8 us  [local(): lax.all_to_all(grads.reshape(1, local_experts, owners * capacity, hidden_...]
    reduce_scatter x2, waiting for transfers between devices: 105 us -> 112 us  [local(): lax.psum_scatter(part, 'dp', scatter_dimension=0, tiled=True)]
    all_to_all x1, blocking collectives: 46.5 us -> 39.1 us  [local(): lax.all_to_all(h_send, 'expert', split_axis=0, concat_axis=2, tiled=True)[0]]
  transfers between devices with their start and end apart: 5 -> 19, of which waited for: 5 -> 17; matrix products, arithmetic and copies ran while one was open for 10% -> 13% of each run, Pallas kernels for 0% -> 0%
where the time goes in v1:
time: 476 us; the launch traced here: 475 us
  waiting for transfers between devices  259 us (54%)
  local copies, waits for them, and re-layouts  88.2 us (19%)
  blocking collectives  62.8 us (13%)
  matrix products  27.4 us (6%)
  other arithmetic  18.8 us (4%)
  between operations  14 us (3%)
  starting transfers between devices  5.59 us (1%)
    ppermute x15, waiting for transfers between devices, gather_by_hops(): terms = [lax.ppermute(terms[0], axis, forward), *terms]  114 us
    reduce_scatter x2, waiting for transfers between devices, local(): lax.psum_scatter(part, 'dp', scatter_dimension=0, tiled=True)  112 us
    unnamed x62, local copies, waits for them, and re-layouts  40.9 us
    all_to_all x1, blocking collectives, local(): lax.all_to_all(h_send, 'expert', split_axis=0, concat_axis=2, tiled=True)[0]  39.1 us
    all_to_all x1, waiting for transfers between devices, local(): lax.all_to_all(grads.reshape(1, local_experts, owners * capacity, hidden_...  31.8 us
    all_gather x1, blocking collectives, local(): lax.all_gather(route_ids.reshape(1, routes), 'expert', axis=0, tiled=True)  23.6 us
    gather x1, local copies, waits for them, and re-layouts, local(): dy_recv = cot_group[rows]  21 us
    dot_general x2, matrix products, local(): jnp.einsum('sf,sd->fd', h_recv[j], dy_recv[j], preferred_element_type=jnp...  12.8 us
  transfers between devices with their start and end apart: 19, of which 17 were waited for; matrix products, arithmetic and copies ran while one was open for 13% of the time, Pallas kernels for 0%

profile of v1, /device:TPU:2, one launch (start us, length us, event | category | flops | bytes accessed | tf_op | source)
XLA Modules:
  0.0 475.4 jit_solution(16396767701264473301)
XLA Ops:
  7.9 11.0 %collective-permute-done = bf16[2,48,2048]{2,1,0:T(8,128)(2,1)S(1)} collective-permute-done((bf16[2,48,2048]{2,1,0:T(8,128)(2,1)}, bf16[2,48,2048]{2,1,0:T(8,128)(2,1)S(1)}, u32[]{:S(2)}, u32[]{:S(2)}) %collective-permute-start) | collective-permute-done | bytes 393248 | tf_op jit(solution)/shard_map/ppermute | solution.py:12
  18.9 8.4 %collective-permute-done.1 = bf16[2,48,2048]{2,1,0:T(8,128)(2,1)S(1)} collective-permute-done((bf16[2,48,2048]{2,1,0:T(8,128)(2,1)S(1)}, bf16[2,48,2048]{2,1,0:T(8,128)(2,1)S(1)}, u32[]{:S(2)}, u32[]{:S(2)}) %collective-permute-start.1) | collective-permute-done | bytes 393248 | tf_op jit(solution)/shard_map/ppermute | solution.py:12
  27.3 8.4 %collective-permute-done.2 = bf16[2,48,2048]{2,1,0:T(8,128)(2,1)S(1)} collective-permute-done((bf16[2,48,2048]{2,1,0:T(8,128)(2,1)S(1)}, bf16[2,48,2048]{2,1,0:T(8,128)(2,1)S(1)}, u32[]{:S(2)}, u32[]{:S(2)}) %collective-permute-start.2) | collective-permute-done | bytes 393248 | tf_op jit(solution)/shard_map/ppermute | solution.py:12
  35.7 8.4 %collective-permute-done.3 = bf16[2,48,2048]{2,1,0:T(8,128)(2,1)S(1)} collective-permute-done((bf16[2,48,2048]{2,1,0:T(8,128)(2,1)S(1)}, bf16[2,48,2048]{2,1,0:T(8,128)(2,1)S(1)}, u32[]{:S(2)}, u32[]{:S(2)}) %collective-permute-start.3) | collective-permute-done | bytes 393248 | tf_op jit(solution)/shard_map/ppermute | solution.py:12
  44.1 8.4 %collective-permute-done.4 = bf16[2,48,2048]{2,1,0:T(8,128)(2,1)S(1)} collective-permute-done((bf16[2,48,2048]{2,1,0:T(8,128)(2,1)S(1)}, bf16[2,48,2048]{2,1,0:T(8,128)(2,1)S(1)}, u32[]{:S(2)}, u32[]{:S(2)}) %collective-permute-start.4) | collective-permute-done | bytes 393248 | tf_op jit(solution)/shard_map/ppermute | solution.py:12
  52.5 8.4 %collective-permute-done.5 = bf16[2,48,2048]{2,1,0:T(8,128)(2,1)S(1)} collective-permute-done((bf16[2,48,2048]{2,1,0:T(8,128)(2,1)S(1)}, bf16[2,48,2048]{2,1,0:T(8,128)(2,1)S(1)}, u32[]{:S(2)}, u32[]{:S(2)}) %collective-permute-start.5) | collective-permute-done | bytes 393248 | tf_op jit(solution)/shard_map/ppermute | solution.py:12
  61.0 8.4 %collective-permute-done.6 = bf16[2,48,2048]{2,1,0:T(8,128)(2,1)S(1)} collective-permute-done((bf16[2,48,2048]{2,1,0:T(8,128)(2,1)S(1)}, bf16[2,48,2048]{2,1,0:T(8,128)(2,1)S(1)}, u32[]{:S(2)}, u32[]{:S(2)}) %collective-permute-start.6) | collective-permute-done | bytes 393248 | tf_op jit(solution)/shard_map/ppermute | solution.py:12
  69.4 8.4 %collective-permute-done.7 = bf16[2,48,2048]{2,1,0:T(8,128)(2,1)S(1)} collective-permute-done((bf16[2,48,2048]{2,1,0:T(8,128)(2,1)S(1)}, bf16[2,48,2048]{2,1,0:T(8,128)(2,1)S(1)}, u32[]{:S(2)}, u32[]{:S(2)}) %collective-permute-start.7) | collective-permute-done | bytes 393248 | tf_op jit(solution)/shard_map/ppermute | solution.py:12
  77.8 8.4 %collective-permute-done.8 = bf16[2,48,2048]{2,1,0:T(8,128)(2,1)S(1)} collective-permute-done((bf16[2,48,2048]{2,1,0:T(8,128)(2,1)S(1)}, bf16[2,48,2048]{2,1,0:T(8,128)(2,1)S(1)}, u32[]{:S(2)}, u32[]{:S(2)}) %collective-permute-start.8) | collective-permute-done | bytes 393248 | tf_op jit(solution)/shard_map/ppermute | solution.py:12
  86.9 8.4 %collective-permute-done.9 = bf16[2,48,2048]{2,1,0:T(8,128)(2,1)S(1)} collective-permute-done((bf16[2,48,2048]{2,1,0:T(8,128)(2,1)S(1)}, bf16[2,48,2048]{2,1,0:T(8,128)(2,1)S(1)}, u32[]{:S(2)}, u32[]{:S(2)}) %collective-permute-start.9) | collective-permute-done | bytes 393248 | tf_op jit(solution)/shard_map/ppermute | solution.py:12
  95.4 1.4 copy.30
  97.7 23.6 %all-gather = s32[16,1,1024]{2,1,0:T(1,128)S(1)} all-gather(s32[1,1,1024]{2,1,0:T(1,128)S(1)} %reshape.205), channel_id=1, replica_groups=mesh['dp'=16,'expert'=16] {'expert'}, dimensions={0}, use_global_device_ids=true | all-gather | bytes 69632 | tf_op jit(solution)/shard_map/all_gather | solution.py:38
  122.6 2.9 fusion.31
  125.5 5.8 %collective-permute-done.11 = bf16[2,48,2048]{2,1,0:T(8,128)(2,1)} collective-permute-done((bf16[2,48,2048]{2,1,0:T(8,128)(2,1)}, bf16[2,48,2048]{2,1,0:T(8,128)(2,1)}, u32[]{:S(2)}, u32[]{:S(2)}) %collective-permute-start.11) | collective-permute-done | bytes 393248 | tf_op jit(solution)/shard_map/ppermute | solution.py:12
  132.4 7.7 %collective-permute-done.12 = bf16[2,48,2048]{2,1,0:T(8,128)(2,1)} collective-permute-done((bf16[2,48,2048]{2,1,0:T(8,128)(2,1)}, bf16[2,48,2048]{2,1,0:T(8,128)(2,1)}, u32[]{:S(2)}, u32[]{:S(2)}) %collective-permute-start.12) | collective-permute-done | bytes 393248 | tf_op jit(solution)/shard_map/ppermute | solution.py:12
  140.1 1.6 select_reduce_fusion.1
  143.2 5.6 %collective-permute-done.13 = bf16[2,48,2048]{2,1,0:T(8,128)(2,1)} collective-permute-done((bf16[2,48,2048]{2,1,0:T(8,128)(2,1)}, bf16[2,48,2048]{2,1,0:T(8,128)(2,1)}, u32[]{:S(2)}, u32[]{:S(2)}) %collective-permute-start.13) | collective-permute-done | bytes 393248 | tf_op jit(solution)/shard_map/ppermute | solution.py:12
  149.5 7.9 %collective-permute-done.14 = bf16[2,48,2048]{2,1,0:T(8,128)(2,1)S(1)} collective-permute-done((bf16[2,48,2048]{2,1,0:T(8,128)(2,1)}, bf16[2,48,2048]{2,1,0:T(8,128)(2,1)S(1)}, u32[]{:S(2)}, u32[]{:S(2)}) %collective-permute-start.14) | collective-permute-done | bytes 393248 | tf_op jit(solution)/shard_map/ppermute | solution.py:12
  158.2 1.8 constant_dynamic-update-slice_fusion.30
  160.0 1.8 constant_dynamic-update-slice_fusion.29
  161.8 1.8 constant_dynamic-update-slice_fusion.28
  163.6 1.8 constant_dynamic-update-slice_fusion.27
  165.4 1.8 constant_dynamic-update-slice_fusion.26
  167.1 1.7 constant_dynamic-update-slice_fusion.25
  176.7 1.8 constant_dynamic-update-slice_fusion.14
  178.5 1.8 constant_dynamic-update-slice_fusion.13
  180.2 1.8 constant_dynamic-update-slice_fusion.12
  182.0 1.8 constant_dynamic-update-slice_fusion.11
  192.4 21.0 %gather_fusion = bf16[2048,2048]{1,0:T(8,128)(2,1)} fusion(bf16[2048,2048]{1,0:T(8,128)(2,1)} %all-gather.3.cloned.1.call-done, s32[2048]{0:T(1024)S(1)} %bitcast_clamp_fusion), kind=kCustom, calls=%fused_computation | custom fusion | bytes 16785408 | tf_op jit(solution)/shard_map/gather | solution.py:74
  213.3 11.2 %convert_bitcast_fusion = bf16[1,2,1024,768]{3,2,1,0:T(8,128)(2,1)S(1)} fusion(bf16[2,1024,2048]{2,1,0:T(8,128)(2,1)} %bitcast.54, bf16[2,1536,2048]{2,1,0:T(8,128)(2,1)} %constant_dynamic-update-slice_fusion, s32[]{:T(128)S(6)} %select_n.69), kind=kOutput, calls=%fused_computation.40 | convolution fusion | flops 6444023808 | bytes 17825796 | tf_op jit(solution)/shard_map/jsd,jfd->jsf/dot_general | solution.py:76
  224.5 4.9 %copy.32 = bf16[1,2,1024,768]{3,1,0,2:T(2,128)(2,1)} copy(bf16[1,2,1024,768]{3,2,1,0:T(8,128)(2,1)S(1)} %convert_bitcast_fusion) | data formatting | bytes 6291456 | tf_op jit(solution)/shard_map/reshape | solution.py:80
  229.4 5.4 %all-to-all-start = ((bf16[1,2,1024,768]{3,1,0,2:T(2,128)(2,1)}), bf16[1,2,1024,768]{3,1,0,2:T(2,128)(2,1)S(1)}, u32[]{:S(2)}, u32[]{:S(2)}) async-start(bf16[1,2,1024,768]{3,1,0,2:T(2,128)(2,1)} %copy.32), calls=%async_computation | async-start | bytes 6291456 | tf_op jit(solution)/shard_map/all_to_all | solution.py:79
  235.9 1.0 fusion
  238.0 31.8 %all-to-all-done = bf16[1,2,1024,768]{3,1,0,2:T(2,128)(2,1)S(1)} async-done(((bf16[1,2,1024,768]{3,1,0,2:T(2,128)(2,1)}), bf16[1,2,1024,768]{3,1,0,2:T(2,128)(2,1)S(1)}, u32[]{:S(2)}, u32[]{:S(2)}) %all-to-all-start) | async-done | bytes 3145760 | tf_op jit(solution)/shard_map/all_to_all | solution.py:79
  269.8 1.7 copy-done.1
  271.5 2.5 copy.33
  274.0 5.4 %gather_fusion.1 = bf16[1024,768]{1,0:T(8,128)(2,1)} fusion(bf16[2048,768]{1,0:T(8,128)(2,1)S(1)} %bitcast.50, s32[1024]{0:T(1024)S(1)} %broadcast_clamp_fusion.1), kind=kCustom, calls=%fused_computation.1 | custom fusion | bytes 3149824 | tf_op jit(solution)/shard_map/gather | solution.py:95
  279.4 5.1 %fusion.33 = (bf16[1024,768]{1,0:T(8,128)(2,1)S(1)}, bf16[128,8,768]{2,1,0:T(8,128)(2,1)S(1)}, bf16[128,8,768]{2,1,0:T(8,128)(2,1)}, bf16[128,8,768]{2,1,0:T(8,128)(2,1)}) fusion(f32[128,8]{1,0:T(8,128)S(1)} %copy.29, bf16[128,8,1536]{2,1,0:T(8,128)(2,1)} %param.6, bf16[1024,768]{1,0:T(8,128)(2,1)} %gather_fusion.1), kind=kLoop, calls=%fused_computation.46 | loop fusion | flops 17301504 | bytes 11014144 | tf_op jit(solution)/shard_map/reshape | solution.py:58
  284.5 9.4 %gather_fusion.2 = bf16[2048,768]{1,0:T(8,128)(2,1)} fusion(bf16[1024,768]{1,0:T(8,128)(2,1)S(1)} %get-tuple-element.9, s32[2048]{0:T(1024)S(1)} %broadcast_clamp_fusion), kind=kCustom, calls=%fused_computation.2 | custom fusion | bytes 6299648 | tf_op jit(solution)/shard_map/gather | solution.py:58
  293.9 2.3 broadcast_select_fusion
  296.2 39.1 %all_to_all.30 = bf16[16,2,64,768]{3,2,1,0:T(8,128)(2,1)S(1)} all-to-all(bf16[16,2,64,768]{3,2,1,0:T(8,128)(2,1)S(1)} %broadcast_select_fusion), channel_id=1, replica_groups=mesh['dp'=16,'expert'=16] {'expert'}, dimensions={0} | all-to-all | bytes 6291456 | tf_op jit(solution)/shard_map/all_to_all | solution.py:75
  335.3 1.4 fusion.47
  336.7 4.9 %fusion.12 = bf16[768,2048]{1,0:T(8,128)(2,1)} fusion(bf16[1024,768]{1,0:T(8,128)(2,1)S(1)} %bitcast.58, bf16[2048,2048]{1,0:T(8,128)(2,1)S(1)} %bitcast.56), kind=kOutput, calls=%fused_computation.26 | convolution fusion | flops 3222798336 | bytes 8912896 | tf_op jit(solution)/shard_map/sf,sd->fd/dot_general | solution.py:88
  341.6 7.9 %fusion.15 = bf16[768,2048]{1,0:T(8,128)(2,1)} fusion(bf16[1024,768]{1,0:T(8,128)(2,1)} %bitcast.57, bf16[2048,2048]{1,0:T(8,128)(2,1)} %gather_fusion), kind=kOutput, calls=%fused_computation.27 | convolution fusion | flops 3222798336 | bytes 8912896 | tf_op jit(solution)/shard_map/sf,sd->fd/dot_general | solution.py:88
  350.7 3.8 pad_maximum_fusion
  354.5 50.4 %reduce-scatter.3.cloned.1.call-done = bf16[48,2048]{1,0:T(8,128)(2,1)} async-done(((bf16[768,2048]{1,0:T(8,128)(2,1)}), bf16[48,2048]{1,0:T(8,128)(2,1)}) %reduce-scatter.3.cloned.1.call-update) | async-done | bytes 196624 | tf_op jit(solution)/shard_map/reduce_scatter | solution.py:92
  404.9 62.1 %reduce-scatter.5.cloned.1.call-done = bf16[48,2048]{1,0:T(8,128)(2,1)} async-done(((bf16[768,2048]{1,0:T(8,128)(2,1)}), bf16[48,2048]{1,0:T(8,128)(2,1)}) %reduce-scatter.5.cloned.1.call-update) | async-done | bytes 196624 | tf_op jit(solution)/shard_map/reduce_scatter | solution.py:92
  467.0 2.0 maximum_convert_fusion
  (101 shorter events, 27.5 us)
Async XLA Ops:
  7.2 185.2 %all-gather.3.cloned.1.call-start = ((), (), s32[]{:S(2)}) async-start(), calls=%async_computation.4 | async-start | bytes 8912896 | tf_op jit(solution)/shard_map/all_gather | solution.py:37
  7.9 11.0 %collective-permute-start = (bf16[2,48,2048]{2,1,0:T(8,128)(2,1)}, bf16[2,48,2048]{2,1,0:T(8,128)(2,1)S(1)}, u32[]{:S(2)}, u32[]{:S(2)}) collective-permute-start(bf16[2,48,2048]{2,1,0:T(8,128)(2,1)} %param.9), channel_id=1, source_target_pairs={{0,16},{16,32},{32,48},{48,64},{64,80},{80,96},{96,112},{112,128},... | collective-permute-start | bytes 1179656 | tf_op jit(solution)/shard_map/ppermute | solution.py:12
  18.9 8.4 %collective-permute-start.1 = (bf16[2,48,2048]{2,1,0:T(8,128)(2,1)S(1)}, bf16[2,48,2048]{2,1,0:T(8,128)(2,1)S(1)}, u32[]{:S(2)}, u32[]{:S(2)}) collective-permute-start(bf16[2,48,2048]{2,1,0:T(8,128)(2,1)S(1)} %collective-permute-done), channel_id=1, source_target_pairs={{0,16},{16,32},{32,48},{48,64},{64,80},{80,96},{96,112},{112,128},... | collective-permute-start | bytes 1179656 | tf_op jit(solution)/shard_map/ppermute | solution.py:12
  27.3 8.4 %collective-permute-start.2 = (bf16[2,48,2048]{2,1,0:T(8,128)(2,1)S(1)}, bf16[2,48,2048]{2,1,0:T(8,128)(2,1)S(1)}, u32[]{:S(2)}, u32[]{:S(2)}) collective-permute-start(bf16[2,48,2048]{2,1,0:T(8,128)(2,1)S(1)} %collective-permute-done.1), channel_id=1, source_target_pairs={{0,16},{16,32},{32,48},{48,64},{64,80},{80,96},{96,112},{112,128},... | collective-permute-start | bytes 1179656 | tf_op jit(solution)/shard_map/ppermute | solution.py:12
  35.7 8.4 %collective-permute-start.3 = (bf16[2,48,2048]{2,1,0:T(8,128)(2,1)S(1)}, bf16[2,48,2048]{2,1,0:T(8,128)(2,1)S(1)}, u32[]{:S(2)}, u32[]{:S(2)}) collective-permute-start(bf16[2,48,2048]{2,1,0:T(8,128)(2,1)S(1)} %collective-permute-done.2), channel_id=1, source_target_pairs={{0,16},{16,32},{32,48},{48,64},{64,80},{80,96},{96,112},{112,128},... | collective-permute-start | bytes 1179656 | tf_op jit(solution)/shard_map/ppermute | solution.py:12
  44.1 8.4 %collective-permute-start.4 = (bf16[2,48,2048]{2,1,0:T(8,128)(2,1)S(1)}, bf16[2,48,2048]{2,1,0:T(8,128)(2,1)S(1)}, u32[]{:S(2)}, u32[]{:S(2)}) collective-permute-start(bf16[2,48,2048]{2,1,0:T(8,128)(2,1)S(1)} %collective-permute-done.3), channel_id=1, source_target_pairs={{0,16},{16,32},{32,48},{48,64},{64,80},{80,96},{96,112},{112,128},... | collective-permute-start | bytes 1179656 | tf_op jit(solution)/shard_map/ppermute | solution.py:12
  52.5 8.4 %collective-permute-start.5 = (bf16[2,48,2048]{2,1,0:T(8,128)(2,1)S(1)}, bf16[2,48,2048]{2,1,0:T(8,128)(2,1)S(1)}, u32[]{:S(2)}, u32[]{:S(2)}) collective-permute-start(bf16[2,48,2048]{2,1,0:T(8,128)(2,1)S(1)} %collective-permute-done.4), channel_id=1, source_target_pairs={{0,16},{16,32},{32,48},{48,64},{64,80},{80,96},{96,112},{112,128},... | collective-permute-start | bytes 1179656 | tf_op jit(solution)/shard_map/ppermute | solution.py:12
  60.9 8.4 %collective-permute-start.6 = (bf16[2,48,2048]{2,1,0:T(8,128)(2,1)S(1)}, bf16[2,48,2048]{2,1,0:T(8,128)(2,1)S(1)}, u32[]{:S(2)}, u32[]{:S(2)}) collective-permute-start(bf16[2,48,2048]{2,1,0:T(8,128)(2,1)S(1)} %collective-permute-done.5), channel_id=1, source_target_pairs={{0,16},{16,32},{32,48},{48,64},{64,80},{80,96},{96,112},{112,128},... | collective-permute-start | bytes 1179656 | tf_op jit(solution)/shard_map/ppermute | solution.py:12
  69.4 8.4 %collective-permute-start.7 = (bf16[2,48,2048]{2,1,0:T(8,128)(2,1)S(1)}, bf16[2,48,2048]{2,1,0:T(8,128)(2,1)S(1)}, u32[]{:S(2)}, u32[]{:S(2)}) collective-permute-start(bf16[2,48,2048]{2,1,0:T(8,128)(2,1)S(1)} %collective-permute-done.6), channel_id=1, source_target_pairs={{0,16},{16,32},{32,48},{48,64},{64,80},{80,96},{96,112},{112,128},... | collective-permute-start | bytes 1179656 | tf_op jit(solution)/shard_map/ppermute | solution.py:12
  77.8 8.4 %collective-permute-start.8 = (bf16[2,48,2048]{2,1,0:T(8,128)(2,1)S(1)}, bf16[2,48,2048]{2,1,0:T(8,128)(2,1)S(1)}, u32[]{:S(2)}, u32[]{:S(2)}) collective-permute-start(bf16[2,48,2048]{2,1,0:T(8,128)(2,1)S(1)} %collective-permute-done.7), channel_id=1, source_target_pairs={{0,16},{16,32},{32,48},{48,64},{64,80},{80,96},{96,112},{112,128},... | collective-permute-start | bytes 1179656 | tf_op jit(solution)/shard_map/ppermute | solution.py:12
  86.2 0.7 copy-start.3
  86.9 8.4 %collective-permute-start.9 = (bf16[2,48,2048]{2,1,0:T(8,128)(2,1)S(1)}, bf16[2,48,2048]{2,1,0:T(8,128)(2,1)S(1)}, u32[]{:S(2)}, u32[]{:S(2)}) collective-permute-start(bf16[2,48,2048]{2,1,0:T(8,128)(2,1)S(1)} %collective-permute-done.8), channel_id=1, source_target_pairs={{0,16},{16,32},{32,48},{48,64},{64,80},{80,96},{96,112},{112,128},... | collective-permute-start | bytes 1179656 | tf_op jit(solution)/shard_map/ppermute | solution.py:12
  95.3 27.3 %copy-start.5 = (bf16[2,48,2048]{2,1,0:T(8,128)(2,1)}, bf16[2,48,2048]{2,1,0:T(8,128)(2,1)S(1)}, u32[]{:S(2)}) copy-start(bf16[2,48,2048]{2,1,0:T(8,128)(2,1)S(1)} %collective-permute-done.9) | copy-start | bytes 1179652
  95.3 27.3 %collective-permute-start.10 = (bf16[2,48,2048]{2,1,0:T(8,128)(2,1)S(1)}, bf16[2,48,2048]{2,1,0:T(8,128)(2,1)}, u32[]{:S(2)}, u32[]{:S(2)}) collective-permute-start(bf16[2,48,2048]{2,1,0:T(8,128)(2,1)S(1)} %collective-permute-done.9), channel_id=1, source_target_pairs={{0,16},{16,32},{32,48},{48,64},{64,80},{80,96},{96,112},{112,128},... | collective-permute-start | bytes 1179656 | tf_op jit(solution)/shard_map/ppermute | solution.py:12
  121.4 0.6 copy-start.7
  122.6 8.7 %collective-permute-start.11 = (bf16[2,48,2048]{2,1,0:T(8,128)(2,1)}, bf16[2,48,2048]{2,1,0:T(8,128)(2,1)}, u32[]{:S(2)}, u32[]{:S(2)}) collective-permute-start(bf16[2,48,2048]{2,1,0:T(8,128)(2,1)} %collective-permute-done.10), channel_id=1, source_target_pairs={{0,16},{16,32},{32,48},{48,64},{64,80},{80,96},{96,112},{112,128},... | collective-permute-start | bytes 1179656 | tf_op jit(solution)/shard_map/ppermute | solution.py:12
  122.6 52.5 %copy-start.2 = (bf16[2,48,2048]{2,1,0:T(8,128)(2,1)S(1)}, bf16[2,48,2048]{2,1,0:T(8,128)(2,1)}, u32[]{:S(2)}) copy-start(bf16[2,48,2048]{2,1,0:T(8,128)(2,1)} %param.9) | copy-start | bytes 1179652
  131.3 8.7 %collective-permute-start.12 = (bf16[2,48,2048]{2,1,0:T(8,128)(2,1)}, bf16[2,48,2048]{2,1,0:T(8,128)(2,1)}, u32[]{:S(2)}, u32[]{:S(2)}) collective-permute-start(bf16[2,48,2048]{2,1,0:T(8,128)(2,1)} %collective-permute-done.11), channel_id=1, source_target_pairs={{0,16},{16,32},{32,48},{48,64},{64,80},{80,96},{96,112},{112,128},... | collective-permute-start | bytes 1179656 | tf_op jit(solution)/shard_map/ppermute | solution.py:12
  140.1 8.7 %collective-permute-start.13 = (bf16[2,48,2048]{2,1,0:T(8,128)(2,1)}, bf16[2,48,2048]{2,1,0:T(8,128)(2,1)}, u32[]{:S(2)}, u32[]{:S(2)}) collective-permute-start(bf16[2,48,2048]{2,1,0:T(8,128)(2,1)} %collective-permute-done.12), channel_id=1, source_target_pairs={{0,16},{16,32},{32,48},{48,64},{64,80},{80,96},{96,112},{112,128},... | collective-permute-start | bytes 1179656 | tf_op jit(solution)/shard_map/ppermute | solution.py:12
  143.2 40.6 %copy-start.6 = (bf16[2,48,2048]{2,1,0:T(8,128)(2,1)S(1)}, bf16[2,48,2048]{2,1,0:T(8,128)(2,1)}, u32[]{:S(2)}) copy-start(bf16[2,48,2048]{2,1,0:T(8,128)(2,1)} %copy-done.5) | copy-start | bytes 1179652
  148.8 8.6 %collective-permute-start.14 = (bf16[2,48,2048]{2,1,0:T(8,128)(2,1)}, bf16[2,48,2048]{2,1,0:T(8,128)(2,1)S(1)}, u32[]{:S(2)}, u32[]{:S(2)}) collective-permute-start(bf16[2,48,2048]{2,1,0:T(8,128)(2,1)} %collective-permute-done.13), channel_id=1, source_target_pairs={{0,16},{16,32},{32,48},{48,64},{64,80},{80,96},{96,112},{112,128},... | collective-permute-start | bytes 1179656 | tf_op jit(solution)/shard_map/ppermute | solution.py:12
  158.2 26.4 %copy-start.4 = (bf16[2,48,2048]{2,1,0:T(8,128)(2,1)S(1)}, bf16[2,48,2048]{2,1,0:T(8,128)(2,1)}, u32[]{:S(2)}) copy-start(bf16[2,48,2048]{2,1,0:T(8,128)(2,1)} %copy-done.3) | copy-start | bytes 1179652
  224.5 10.4 %copy-start.8 = (s32[128,8]{1,0:T(8,128)S(1)}, s32[128,8]{1,0:T(8,128)}, u32[]{:S(2)}) copy-start(s32[128,8]{1,0:T(8,128)} %copy.30) | copy-start | bytes 12292
  224.5 11.1 %copy-start.9 = (s32[128,8]{0,1:T(8,128)S(1)}, s32[128,8]{0,1:T(8,128)}, u32[]{:S(2)}) copy-start(s32[128,8]{0,1:T(8,128)} %param.7) | copy-start | bytes 12292
  224.5 11.3 %copy-start.10 = (f32[128,8]{0,1:T(8,128)S(1)}, f32[128,8]{0,1:T(8,128)}, u32[]{:S(2)}) copy-start(f32[128,8]{0,1:T(8,128)} %param.8) | copy-start | bytes 12292
  229.4 40.4 %all-to-all-start = ((bf16[1,2,1024,768]{3,1,0,2:T(2,128)(2,1)}), bf16[1,2,1024,768]{3,1,0,2:T(2,128)(2,1)S(1)}, u32[]{:S(2)}, u32[]{:S(2)}) async-start(bf16[1,2,1024,768]{3,1,0,2:T(2,128)(2,1)} %copy.32), calls=%async_computation | async-start | bytes 6291456 | tf_op jit(solution)/shard_map/all_to_all | solution.py:79
  234.8 170.0 %reduce-scatter.3.cloned.1.call-start = ((), (), s32[]{:S(2)}) async-start(), calls=%async_computation.5 | async-start | bytes 3342336 | tf_op jit(solution)/shard_map/reduce_scatter | solution.py:92
  269.8 1.7 copy-start.1
  293.9 42.8 %slice-start = ((s8[8388608]{0:T(1024)(128)(4,1)}), s8[4194304]{0:T(1024)(128)(4,1)S(1)}, s32[]{:S(2)}) async-start(s8[8388608]{0:T(1024)(128)(4,1)} %bitcast.55), calls=%async_computation.7 | async-start | bytes 8388608
  296.1 40.5 %slice-start.1 = ((s8[8388608]{0:T(1024)(128)(4,1)}), s8[4194304]{0:T(1024)(128)(4,1)S(1)}, s32[]{:S(2)}) async-start(s8[8388608]{0:T(1024)(128)(4,1)} %bitcast.55), calls=%async_computation.8 | async-start | bytes 8388608
  341.5 8.0 %copy-start = (bf16[1024,768]{1,0:T(8,128)(2,1)S(1)}, bf16[1024,768]{1,0:T(8,128)(2,1)}, u32[]{:S(2)}) copy-start(bf16[1024,768]{1,0:T(8,128)(2,1)} %gather_fusion.1) | copy-start | bytes 4718596
  341.6 125.4 %reduce-scatter.5.cloned.1.call-start = ((), (), s32[]{:S(2)}) async-start(), calls=%async_computation.6 | async-start | bytes 3342336 | tf_op jit(solution)/shard_map/reduce_scatter | solution.py:92
Sparse Core Ops, SparseCore 0:
  10.4 78.6 all-gather.2
  341.7 63.1 reduce-scatter.2
  407.4 59.4 reduce-scatter.4
